TPU v7x, 32 devices: a whole 2x2x4 slice. The times are simulated.
32 devices in a mesh: req: 8 (over z, y), tp: 4 (over x, core).
Axes of the slice: x: 2, y: 2, z: 4, core: 2. Of those that a mesh axis runs over, the one named last changes fastest.
Arguments:
- hidden_in: bfloat16 [512, 2048], P('req'), may hold values from -6 to 6
- queries: bfloat16 [512, 2048], P('req', 'tp'), may hold values from -200 to 200, as said below
- keys_new: bfloat16 [512, 2048], P('req', 'tp'), may hold values from -6 to 6
- values_new: bfloat16 [512, 2048], P('req', 'tp'), may hold values from -6 to 6
- prefix_keys: bfloat16 [8, 16, 2048], P('req', None, 'tp'), may hold values from -6 to 6
- prefix_values: bfloat16 [8, 16, 2048], P('req', None, 'tp'), may hold values from -6 to 6
- block_group: int32 [8], P('req'), may hold values from 0 to 1, as said below
- req_group: int32 [8], P('req'), may hold values from 0 to 1
- lengths: int32 [8], P('req'), may hold values from 1 to 64, 320 in all
- w_out: bfloat16 [2048, 2048], P('tp'), may hold values from -0.125 to 0.125
- norm_gain: bfloat16 [2048], replicated, may hold values from 0.25 to 1.75
- w_router: float32 [2048, 64], replicated, may hold values from -7 to 7
- routes: int32 [512, 8], P('req'), may hold values from 0 to 63, all different within a row; in each aligned block of 64 rows (0 to 63, 64 to 127, ...) at most 10 rows name the same one
- w_gate: bfloat16 [128, 2048, 512], P('req', None, 'tp'), may hold values from -0.125 to 0.125
- w_up: bfloat16 [128, 2048, 512], P('req', None, 'tp'), may hold values from -0.125 to 0.125
- w_down: bfloat16 [128, 512, 2048], P('req', 'tp'), may hold values from -0.1875 to 0.1875
Outputs:
- layer_out: bfloat16 [512, 2048], P('req', 'tp')
Inputs may be any that keep to these rules, and one draw needn't show every extreme that they name: queries: the printed draw and the hidden one differ in row scales. `block_group`: exactly half of the 8 cache blocks belong to each group. `routes`: within the rows of one request, each expert is named by at most 10 rows, a bound that some block reaches. `lengths`: each request has at least one live suffix slot, and some request has all 64.
All inputs are finite; a program needn't handle non-finite values. No bound on the sum of `lengths` on one device may be relied on, other than what follows from the above.
Results may differ from a plain program's by a relative error of at most 0.025.
Values may be sent and summed in bfloat16 or wider, within the bound.
A program may use at most 128 MiB of HBM per device.

v0:
```python
import math
import jax
import jax.numpy as jnp
from jax import lax
from jax.sharding import PartitionSpec as P

HD = 128
E = 64
TOPK = 8
CAP = 10
epsilon = 1e-06


def slot_numbers(block_routes):
    flatten = block_routes.reshape(-1)
    chosen = (flatten[:, None] == jnp.arange(E, dtype=jnp.int32)[None, :]).astype(jnp.int32)
    earlier = jnp.cumsum(chosen, axis=0) - chosen
    return (flatten, jnp.sum(earlier * chosen, axis=1))


def body(
    hidden_in,
    queries,
    keys_new,
    values_new,
    prefix_keys,
    prefix_values,
    block_group,
    req_group,
    lengths,
    w_out,
    norm_gain,
    w_router,
    routes,
    w_gate,
    w_up,
    w_down,
):
    row_count = queries.shape[0]
    local_heads = queries.shape[1] // HD
    width = hidden_in.shape[1]
    factor = 1.0 / math.sqrt(HD)
    query_rows = queries.reshape(row_count, local_heads, HD)
    key_rows = keys_new.reshape(row_count, local_heads, HD)
    value_rows = values_new.reshape(row_count, local_heads, HD)
    group_id = req_group[0].astype(jnp.float32)
    own_valid = jnp.arange(row_count) < lengths[0]
    scores = (
        jnp.einsum("qhd,khd->hqk", query_rows, key_rows, preferred_element_type=jnp.float32)
        * factor
    )
    scores = jnp.where(own_valid[None, None, :], scores, -jnp.inf)
    top_score = jnp.max(scores, axis=-1)
    weights = jnp.exp(scores - top_score[..., None])
    best = top_score
    total = jnp.sum(weights, axis=-1)
    summed = jnp.einsum(
        "hqk,khd->hqd", weights.astype(jnp.bfloat16), value_rows, preferred_element_type=jnp.float32
    )
    piece_keys = lax.all_gather(prefix_keys, "req", axis=0, tiled=True)
    piece_values = lax.all_gather(prefix_values, "req", axis=0, tiled=True)
    piece_groups = lax.all_gather(block_group.astype(jnp.bfloat16), "req", axis=0, tiled=True)
    count = piece_keys.shape[0] * piece_keys.shape[1]
    flat_keys = piece_keys.reshape(count, local_heads, HD)
    flat_values = piece_values.reshape(count, local_heads, HD)
    key_valid = jnp.repeat(piece_groups.astype(jnp.float32), piece_keys.shape[1]) == group_id
    block_scores = (
        jnp.einsum("qhd,khd->hqk", query_rows, flat_keys, preferred_element_type=jnp.float32)
        * factor
    )
    block_scores = jnp.where(key_valid[None, None, :], block_scores, -jnp.inf)
    new_best = jnp.maximum(best, jnp.max(block_scores, axis=-1))
    shrink = jnp.exp(best - new_best)
    block_weights = jnp.exp(block_scores - new_best[..., None])
    added = jnp.einsum(
        "hqk,khd->hqd",
        block_weights.astype(jnp.bfloat16),
        flat_values,
        preferred_element_type=jnp.float32,
    )
    best, total, summed = (
        new_best,
        total * shrink + jnp.sum(block_weights, axis=-1),
        summed * shrink[..., None] + added,
    )
    mixed = (summed / total[..., None]).astype(jnp.bfloat16)
    mixed = jnp.transpose(mixed, (1, 0, 2)).reshape(row_count, local_heads * HD)
    partial_value = jnp.dot(mixed, w_out, preferred_element_type=jnp.float32)
    tp_count = lax.axis_size("tp")
    col_width = width // tp_count
    col_start = lax.axis_index("tp") * col_width
    whole = hidden_in.astype(jnp.float32) + lax.psum(
        partial_value.astype(jnp.bfloat16), "tp"
    ).astype(jnp.float32)
    mean_square = jnp.mean(whole * whole, axis=1, keepdims=True)
    normed = (
        whole * lax.rsqrt(mean_square + epsilon) * norm_gain.astype(jnp.float32)[None, :]
    ).astype(jnp.bfloat16)
    state_cols = lax.dynamic_slice_in_dim(whole, col_start, col_width, 1)
    logits = jnp.dot(normed.astype(jnp.float32), w_router, precision=lax.Precision.HIGHEST)
    expert_ids = jnp.arange(E, dtype=jnp.int32)
    picked = jnp.sum(
        jnp.where(routes[:, :, None] == expert_ids[None, None, :], logits[:, None, :], 0.0), axis=2
    )
    gates = jax.nn.softmax(picked, axis=1)
    flatten, slot = slot_numbers(routes)
    position = (flatten * CAP + slot).reshape(row_count, TOPK)
    columns = jnp.arange(E * CAP, dtype=jnp.int32)
    hits = position[:, :, None] == columns[None, None, :]
    placing = jnp.any(hits, axis=1).astype(jnp.bfloat16)
    outgoing = jnp.einsum("tc,td->cd", placing, normed, preferred_element_type=jnp.float32).astype(
        jnp.bfloat16
    )
    combining = jnp.sum(jnp.where(hits, gates[:, :, None], 0.0), axis=1)
    doubled = jnp.repeat(outgoing.reshape(E, CAP, width), 2, axis=0)
    received = lax.all_to_all(doubled, "req", split_axis=0, concat_axis=1, tiled=True)
    gate_val = jnp.einsum("lrd,ldf->lrf", received, w_gate, preferred_element_type=jnp.float32)
    up_val = jnp.einsum("lrd,ldf->lrf", received, w_up, preferred_element_type=jnp.float32)
    inner = (jax.nn.silu(gate_val) * up_val).astype(jnp.bfloat16)
    pieces = jnp.einsum("lrf,lfd->lrd", inner, w_down, preferred_element_type=jnp.float32).astype(
        jnp.bfloat16
    )
    returned = lax.all_to_all(pieces, "req", split_axis=1, concat_axis=0, tiled=True)
    summed_halves = jnp.sum(returned.reshape(E, 2, CAP, width).astype(jnp.float32), axis=1).reshape(
        E * CAP, width
    )
    expert_part = jnp.dot(
        combining,
        summed_halves,
        precision=lax.Precision.HIGHEST,
        preferred_element_type=jnp.float32,
    )
    expert_cols = lax.psum_scatter(
        expert_part.astype(jnp.bfloat16), "tp", scatter_dimension=1, tiled=True
    ).astype(jnp.float32)
    return (state_cols + expert_cols).astype(jnp.bfloat16)


def solution(mesh):
    in_specs = (
        P("req", None),
        P("req", "tp"),
        P("req", "tp"),
        P("req", "tp"),
        P("req", None, "tp"),
        P("req", None, "tp"),
        P("req"),
        P("req"),
        P("req"),
        P("tp", None),
        P(),
        P(),
        P("req", None),
        P("req", None, "tp"),
        P("req", None, "tp"),
        P("req", "tp", None),
    )
    out_specs = P("req", "tp")
    return jax.shard_map(body, mesh=mesh, in_specs=in_specs, out_specs=out_specs, check_vma=False)
```

profile of v0, /device:TPU:0, one launch (start us, length us, event | category | flops | bytes accessed | tf_op | source)
XLA Modules:
  0.0 582.9 jit_solution(14911283072433838208)
XLA Ops:
  6.5 0.0 copy-start
  6.5 0.0 all-reduce.3.cloned.1.call-start
  8.7 1.2 dynamic-slice
  10.0 0.8 dynamic-update-slice
  10.7 23.1 %all-reduce = bf16[8]{0:T(256)(128)(2,1)S(1)} all-reduce(bf16[8]{0:T(256)(128)(2,1)S(1)} %dynamic-update-slice), channel_id=1, replica_groups=mesh['req'=8,'tp'=4] {'req'}, use_global_device_ids=true, to_apply=%add | all-reduce | flops 8 | bytes 32
  33.8 0.1 broadcast_in_dim.72
  33.9 0.1 eq.67
  34.0 30.7 %all_gather.10 = bf16[8,16,512]{2,1,0:T(8,128)(2,1)S(1)} all-gather(bf16[1,16,512]{2,1,0:T(8,128)(2,1)} %param.20), channel_id=1, replica_groups=mesh['req'=8,'tp'=4] {'req'}, dimensions={0}, use_global_device_ids=true | all-gather | bytes 147456 | tf_op jit(solution)/shard_map/all_gather | solution.py:60
  64.8 30.7 %all_gather.11 = bf16[8,16,512]{2,1,0:T(8,128)(2,1)S(1)} all-gather(bf16[1,16,512]{2,1,0:T(8,128)(2,1)} %param.21), channel_id=1, replica_groups=mesh['req'=8,'tp'=4] {'req'}, dimensions={0}, use_global_device_ids=true | all-gather | bytes 147456 | tf_op jit(solution)/shard_map/all_gather | solution.py:61
  95.5 1.1 fusion.57
  96.7 1.1 fusion.56
  97.8 0.2 fusion.34
  98.0 1.1 fusion.14
  99.1 0.2 fusion.19
  99.3 0.0 copy-done
  99.3 1.2 convolution_convert_fusion.3
  100.5 0.0 all-reduce.3.cloned.1.call-update
  100.5 0.0 copy-done.6
  100.5 0.1 copy.95
  100.6 0.1 eq.72
  100.7 0.1 eq.68
  100.8 0.0 copy-done.7
  100.8 1.2 reduce-window.6
  102.0 0.2 slice_reduce_fusion
  102.3 0.1 fusion.28
  102.4 0.1 reduce_sum.83
  102.5 0.1 copy.98
  102.6 0.1 copy.99
  102.7 0.5 fusion.4
  103.2 26.7 %all-reduce.3.cloned.1.call-done = bf16[64,2048]{1,0:T(8,128)(2,1)} async-done(((bf16[64,2048]{1,0:T(8,128)(2,1)}), bf16[64,2048]{1,0:T(8,128)(2,1)}) %all-reduce.3.cloned.1.call-update) | async-done | bytes 262160 | tf_op jit(solution)/shard_map/psum | solution.py:92
  129.9 0.0 copy-done.3
  129.9 1.1 convert_add_fusion
  131.0 3.4 convolution_convert_fusion.1
  134.4 5.4 reshape.145
  139.8 6.8 %broadcast_in_dim.79 = bf16[64,2,10,2048]{3,2,1,0:T(8,128)(2,1)} broadcast(bf16[64,10,2048]{2,1,0:T(8,128)(2,1)} %reshape.145), dimensions={0,2,3} | broadcast | bytes 7864320 | tf_op jit(solution)/shard_map/broadcast_in_dim | solution.py:115
  146.5 187.4 %all_to_all.27 = bf16[128,10,2048]{2,1,0:T(8,128)(2,1)S(1)} all-to-all(bf16[128,10,2048]{2,1,0:T(8,128)(2,1)} %bitcast.107), channel_id=1, replica_groups=mesh['req'=8,'tp'=4] {'req'}, dimensions={0} | all-to-all | bytes 10485760 | tf_op jit(solution)/shard_map/all_to_all | solution.py:116
  334.0 3.4 copy.105
  337.4 0.0 copy-start.2
  337.4 2.3 copy-done.2
  339.7 9.7 %fusion.2 = f32[16,80,128]{2,1,0:T(8,128)S(1)} fusion(bf16[16,2048,128]{2,1,0:T(8,128)(2,1)} %param.29, bf16[16,80,2048]{2,0,1:T(8,128)(2,1)S(1)} %bitcast.109), kind=kOutput, calls=%fused_computation.3 | convolution fusion | flops 671088640 | bytes 14286848 | tf_op jit(solution)/shard_map/lrd,ldf->lrf/dot_general | solution.py:117
  349.5 17.3 %convolution_convert_fusion = bf16[16,80,2048]{2,1,0:T(8,128)(2,1)} fusion(bf16[16,128,2048]{2,1,0:T(8,128)(2,1)} %param.31, bf16[16,2048,128]{2,1,0:T(8,128)(2,1)} %param.30, bf16[16,80,2048]{2,0,1:T(8,128)(2,1)} %bitcast.110, f32[16,80,128]{2,1,0:T(8,128)S(1)} %fusion.2), kind=kOutput, calls=%fused_computation.5 | convolution fusion | flops 1345781760 | bytes 27918336 | tf_op jit(solution)/shard_map/lrf,lfd->lrd/dot_general | solution.py:120
  366.8 7.7 %copy.108 = bf16[16,80,2048]{2,0,1:T(8,128)(2,1)} copy(bf16[16,80,2048]{2,1,0:T(8,128)(2,1)} %convolution_convert_fusion) | data formatting | bytes 10485760 | tf_op jit(solution)/shard_map/convert_element_type | solution.py:120
  374.5 4.8 all-to-all-start.1
  379.3 0.0 reduce-scatter.2.cloned.1.call-start
  379.3 0.0 copy-done.4
  379.3 0.0 copy-done.5
  379.3 0.5 fusion.54
  379.8 0.2 select_reduce_fusion.1
  380.0 0.1 copy.102
  380.1 0.1 reduce_max.35
  380.2 0.1 copy.103
  380.3 0.5 select_reduce_fusion
  380.8 113.0 %all-to-all-done.1 = bf16[16,80,2048]{2,0,1:T(8,128)(2,1)} async-done(((bf16[16,80,2048]{2,0,1:T(8,128)(2,1)}), bf16[16,80,2048]{2,0,1:T(8,128)(2,1)}, u32[]{:S(2)}, u32[]{:S(2)}) %all-to-all-start.1) | async-done | bytes 5242912 | tf_op jit(solution)/shard_map/all_to_all | solution.py:123
  493.8 3.9 convert_bitcast_fusion
  497.7 4.7 copy.109
  502.4 13.1 %reshape.148 = f32[64,2,10,2048]{3,1,0,2:T(2,128)} reshape(f32[8,16,10,2048]{3,1,0,2:T(8,128)} %copy.109) | data formatting | bytes 20971520 | tf_op jit(solution)/shard_map/convert_element_type | solution.py:124
  515.5 17.0 %reduce_sum.88 = f32[64,10,2048]{2,0,1:T(8,128)} reduce(f32[64,2,10,2048]{3,1,0,2:T(2,128)} %reshape.148, f32[]{:T(128)} %constant.14.clone.1), dimensions={1}, to_apply=%region_14.15 | reduce | flops 1310720 | bytes 15728644 | tf_op jit(solution)/shard_map/reduce_sum | solution.py:124
  532.5 8.9 %copy.110 = f32[64,10,2048]{2,1,0:T(8,128)} copy(f32[64,10,2048]{2,0,1:T(8,128)} %reduce_sum.88) | data formatting | bytes 10485760 | tf_op jit(solution)/shard_map/reduce_sum | solution.py:124
  541.4 7.6 %reshape.147 = f32[640,2048]{1,0:T(8,128)} reshape(f32[64,10,2048]{2,1,0:T(8,128)} %copy.110) | data formatting | bytes 10485760 | tf_op jit(solution)/shard_map/reshape | solution.py:124
  549.0 6.4 %convolution_convert_fusion.2 = bf16[64,2048]{1,0:T(8,128)(2,1)} fusion(f32[64,640]{1,0:T(8,128)S(1)} %select_reduce_fusion, f32[640,2048]{1,0:T(8,128)} %reshape.147), kind=kOutput, calls=%fused_computation.7 | convolution fusion | flops 1006764032 | bytes 5668864 | tf_op jit(solution)/shard_map/dot_general | solution.py:127
  555.4 0.0 reduce-scatter.2.cloned.1.call-update
  555.4 18.9 %reduce-scatter.2.cloned.1.call-done = bf16[64,512]{1,0:T(8,128)(2,1)} async-done(((bf16[64,2048]{1,0:T(8,128)(2,1)}), bf16[64,512]{1,0:T(8,128)(2,1)}) %reduce-scatter.2.cloned.1.call-update) | async-done | bytes 65552 | tf_op jit(solution)/shard_map/reduce_scatter | solution.py:133
  574.3 1.5 add_convert_fusion
  575.8 0.0 copy-done.1
  (22 shorter events, 0.3 us)
Async XLA Ops:
  6.5 92.8 %copy-start = (bf16[512,2048]{1,0:T(8,128)(2,1)S(1)}, bf16[512,2048]{1,0:T(8,128)(2,1)}, u32[]{:S(2)}) copy-start(bf16[512,2048]{1,0:T(8,128)(2,1)} %param.25) | copy-start | bytes 6291460
  6.5 94.0 %copy-start.6 = (s32[64,8]{0,1:T(8,128)S(1)}, s32[64,8]{0,1:T(8,128)}, u32[]{:S(2)}) copy-start(s32[64,8]{0,1:T(8,128)} %param.28) | copy-start | bytes 6148
  6.5 94.2 %copy-start.7 = (bf16[2048]{0:T(1024)(128)(2,1)S(1)}, bf16[2048]{0:T(1024)(128)(2,1)}, u32[]{:S(2)}) copy-start(bf16[2048]{0:T(1024)(128)(2,1)} %param.26) | copy-start | bytes 12292
  6.5 123.3 %copy-start.3 = (bf16[64,2048]{1,0:T(8,128)(2,1)S(1)}, bf16[64,2048]{1,0:T(8,128)(2,1)}, u32[]{:S(2)}) copy-start(bf16[64,2048]{1,0:T(8,128)(2,1)} %param.16) | copy-start | bytes 786436
  6.5 123.3 %all-reduce.3.cloned.1.call-start = ((), (), s32[]{:S(2)}) async-start(), calls=%async_computation.3 | async-start | bytes 524288 | tf_op jit(solution)/shard_map/psum | solution.py:92
  337.4 2.3 copy-start.2
  374.4 4.9 copy-start.4
  374.5 4.9 copy-start.5
  374.5 119.4 %all-to-all-start.1 = ((bf16[16,80,2048]{2,0,1:T(8,128)(2,1)}), bf16[16,80,2048]{2,0,1:T(8,128)(2,1)}, u32[]{:S(2)}, u32[]{:S(2)}) async-start(bf16[16,80,2048]{2,0,1:T(8,128)(2,1)} %copy.108), calls=%async_computation.1 | async-start | bytes 10485760 | tf_op jit(solution)/shard_map/all_to_all | solution.py:123
  379.3 195.1 %reduce-scatter.2.cloned.1.call-start = ((), (), s32[]{:S(2)}) async-start(), calls=%async_computation.4 | async-start | bytes 327680 | tf_op jit(solution)/shard_map/reduce_scatter | solution.py:133
  541.4 34.4 %copy-start.1 = (bf16[512,2048]{1,0:T(8,128)(2,1)S(1)}, bf16[512,2048]{1,0:T(8,128)(2,1)}, u32[]{:S(2)}) copy-start(bf16[512,2048]{1,0:T(8,128)(2,1)} %param.25) | copy-start | bytes 6291460
Sparse Core Ops, SparseCore 0:
  100.6 29.2 all-reduce.2
  555.6 18.7 reduce-scatter.1
where the time goes:
time: 588 us; the launch traced here: 583 us
  blocking collectives  272 us (46%)
  waiting for transfers between devices  159 us (27%)
  local copies, waits for them, and re-layouts  63 us (11%)
  matrix products  41.9 us (7%)
  other arithmetic  26.5 us (5%)
  between operations  16 us (3%)
    all_to_all x1, blocking collectives, body(): lax.all_to_all(doubled, 'req', split_axis=0, concat_axis=1, tiled=True)  187 us
    all_to_all x1, waiting for transfers between devices, body(): lax.all_to_all(pieces, 'req', split_axis=1, concat_axis=0, tiled=True)  113 us
    all_gather x1, blocking collectives, body(): piece_values = lax.all_gather(prefix_values, 'req', axis=0, tiled=True)  30.7 us
    all_gather x1, blocking collectives, body(): piece_keys = lax.all_gather(prefix_keys, 'req', axis=0, tiled=True)  30.7 us
    psum x1, waiting for transfers between devices, body(): lax.psum(partial_value.astype(jnp.bfloat16), 'tp').astype(jnp.float32)  26.7 us
    unnamed x1, blocking collectives  23.1 us
    reduce_scatter x1, waiting for transfers between devices, body(): lax.psum_scatter(expert_part.astype(jnp.bfloat16), 'tp', scatter_dimensio...  18.9 us
    convert_element_type x2, local copies, waits for them, and re-layouts, body(): returned.reshape(E, 2, CAP, width).astype(jnp.float32)  17.8 us
  transfers between devices with their start and end apart: 3, of which 3 were waited for; matrix products, arithmetic and copies ran while one was open for 1% of the time, Pallas kernels for 0%

commit v1 on v0

--- a/solution.py
+++ b/solution.py
@@ -120,7 +120,9 @@
     pieces = jnp.einsum("lrf,lfd->lrd", inner, w_down, preferred_element_type=jnp.float32).astype(
         jnp.bfloat16
     )
-    returned = lax.all_to_all(pieces, "req", split_axis=1, concat_axis=0, tiled=True)
+    returned = jnp.concatenate(
+        lax.all_to_all(jnp.stack(jnp.split(pieces, lax.axis_size("req"), 1)), "req", 0, 0), 0
+    )
     summed_halves = jnp.sum(returned.reshape(E, 2, CAP, width).astype(jnp.float32), axis=1).reshape(
         E * CAP, width
     )

time: 588 us -> 594 us (1.010)
  local copies, waits for them, and re-layouts: 63 us -> 72.8 us
    unnamed x20 -> x25, local copies, waits for them, and re-layouts: 4.42 us -> 13.3 us
    convert_element_type x1 -> x0, local copies, waits for them, and re-layouts: 7.67 us -> none  [body(): jnp.einsum('lrf,lfd->lrd', inner, w_down, preferred_element_type=jnp.floa...]
where the time goes in v1:
time: 594 us; the launch traced here: 588 us
  blocking collectives  272 us (46%)
  waiting for transfers between devices  156 us (26%)
  local copies, waits for them, and re-layouts  72.8 us (12%)
  matrix products  42 us (7%)
  other arithmetic  24 us (4%)
  between operations  16 us (3%)
    all_to_all x1, blocking collectives, body(): lax.all_to_all(doubled, 'req', split_axis=0, concat_axis=1, tiled=True)  187 us
    all_to_all x1, waiting for transfers between devices, body(): lax.all_to_all(jnp.stack(jnp.split(pieces, lax.axis_size('req'), 1)), 're...  113 us
    all_gather x1, blocking collectives, body(): piece_values = lax.all_gather(prefix_values, 'req', axis=0, tiled=True)  30.7 us
    all_gather x1, blocking collectives, body(): piece_keys = lax.all_gather(prefix_keys, 'req', axis=0, tiled=True)  30.7 us
    psum x1, waiting for transfers between devices, body(): lax.psum(partial_value.astype(jnp.bfloat16), 'tp').astype(jnp.float32)  24.7 us
    unnamed x1, blocking collectives  23.1 us
    convert_element_type x2, local copies, waits for them, and re-layouts, body(): returned.reshape(E, 2, CAP, width).astype(jnp.float32)  20.8 us
    reduce_scatter x1, waiting for transfers between devices, body(): lax.psum_scatter(expert_part.astype(jnp.bfloat16), 'tp', scatter_dimensio...  18.8 us
  transfers between devices with their start and end apart: 3, of which 3 were waited for; matrix products, arithmetic and copies ran while one was open for 1% of the time, Pallas kernels for 0%

profile of v1, /device:TPU:0, one launch (start us, length us, event | category | flops | bytes accessed | tf_op | source)
XLA Modules:
  0.0 588.3 jit_solution(4179388420171971236)
XLA Ops:
  6.5 0.0 copy-start
  8.7 1.2 dynamic-slice
  9.9 0.8 dynamic-update-slice
  10.7 23.1 %all-reduce = bf16[8]{0:T(256)(128)(2,1)S(1)} all-reduce(bf16[8]{0:T(256)(128)(2,1)S(1)} %dynamic-update-slice), channel_id=1, replica_groups=mesh['req'=8,'tp'=4] {'req'}, use_global_device_ids=true, to_apply=%add | all-reduce | flops 8 | bytes 32
  33.8 0.1 broadcast_in_dim.72
  33.9 0.1 eq.67
  34.0 30.7 %all_gather.10 = bf16[8,16,512]{2,1,0:T(8,128)(2,1)S(1)} all-gather(bf16[1,16,512]{2,1,0:T(8,128)(2,1)} %param.20), channel_id=1, replica_groups=mesh['req'=8,'tp'=4] {'req'}, dimensions={0}, use_global_device_ids=true | all-gather | bytes 147456 | tf_op jit(solution)/shard_map/all_gather | solution.py:60
  64.7 30.7 %all_gather.11 = bf16[8,16,512]{2,1,0:T(8,128)(2,1)S(1)} all-gather(bf16[1,16,512]{2,1,0:T(8,128)(2,1)} %param.21), channel_id=1, replica_groups=mesh['req'=8,'tp'=4] {'req'}, dimensions={0}, use_global_device_ids=true | all-gather | bytes 147456 | tf_op jit(solution)/shard_map/all_gather | solution.py:61
  95.5 1.1 fusion.65
  96.6 1.0 fusion.64
  97.7 0.2 fusion.42
  97.9 1.1 fusion.14
  99.0 0.2 fusion.19
  99.3 1.2 convolution_convert_fusion.3
  100.4 0.0 all-reduce.3.cloned.1.call-update
  100.5 0.8 copy.132
  101.2 0.1 eq.72
  101.3 0.1 eq.68
  101.4 0.7 convert_element_type.82
  102.1 1.2 reduce-window.6
  103.3 0.2 slice_reduce_fusion
  103.6 0.1 fusion.36
  103.7 0.1 reduce_sum.83
  103.8 0.1 copy.135
  103.9 0.7 multiply_add_fusion
  104.6 0.1 copy.136
  104.7 0.5 fusion.4
  105.1 24.7 %all-reduce.3.cloned.1.call-done = bf16[64,2048]{1,0:T(8,128)(2,1)} async-done(((bf16[64,2048]{1,0:T(8,128)(2,1)}), bf16[64,2048]{1,0:T(8,128)(2,1)}) %all-reduce.3.cloned.1.call-update) | async-done | bytes 262160 | tf_op jit(solution)/shard_map/psum | solution.py:92
  129.8 1.2 convert_add_fusion
  131.1 3.5 convolution_convert_fusion.1
  134.5 5.4 reshape.141
  139.9 6.8 %broadcast_in_dim.79 = bf16[64,2,10,2048]{3,2,1,0:T(8,128)(2,1)} broadcast(bf16[64,10,2048]{2,1,0:T(8,128)(2,1)} %reshape.141), dimensions={0,2,3} | broadcast | bytes 7864320 | tf_op jit(solution)/shard_map/broadcast_in_dim | solution.py:115
  146.7 187.4 %all_to_all.23 = bf16[128,10,2048]{2,1,0:T(8,128)(2,1)S(1)} all-to-all(bf16[128,10,2048]{2,1,0:T(8,128)(2,1)} %bitcast.135), channel_id=1, replica_groups=mesh['req'=8,'tp'=4] {'req'}, dimensions={0} | all-to-all | bytes 10485760 | tf_op jit(solution)/shard_map/all_to_all | solution.py:116
  334.1 3.4 copy.142
  337.5 2.3 copy-done.3
  339.8 9.7 %fusion.2 = f32[16,80,128]{2,1,0:T(8,128)S(1)} fusion(bf16[16,2048,128]{2,1,0:T(8,128)(2,1)} %param.29, bf16[16,80,2048]{2,0,1:T(8,128)(2,1)S(1)} %bitcast.137), kind=kOutput, calls=%fused_computation.2 | convolution fusion | flops 671088640 | bytes 14286848 | tf_op jit(solution)/shard_map/lrd,ldf->lrf/dot_general | solution.py:117
  349.6 17.3 %convolution_convert_fusion = bf16[16,80,2048]{2,1,0:T(8,128)(2,1)} fusion(bf16[16,128,2048]{2,1,0:T(8,128)(2,1)} %param.31, bf16[16,2048,128]{2,1,0:T(8,128)(2,1)} %param.30, bf16[16,80,2048]{2,0,1:T(8,128)(2,1)} %bitcast.138, f32[16,80,128]{2,1,0:T(8,128)S(1)} %fusion.2), kind=kOutput, calls=%fused_computation.4 | convolution fusion | flops 1345781760 | bytes 27918336 | tf_op jit(solution)/shard_map/lrf,lfd->lrd/dot_general | solution.py:120
  366.9 1.4 fusion.27
  368.3 2.2 fusion.26
  370.5 1.8 fusion.25
  372.4 1.8 fusion.24
  374.2 0.1 fusion.23
  374.3 0.4 fusion.22
  374.7 0.4 fusion.21
  375.2 0.3 fusion.20
  375.4 5.3 copy.145
  380.8 4.8 all-to-all-start.1
  385.6 0.3 reduce-scatter.2.cloned.1.call-start
  385.9 0.5 fusion.62
  386.4 0.2 select_reduce_fusion.1
  386.6 0.1 copy.139
  386.7 0.1 reduce_max.35
  386.8 0.1 copy.140
  386.9 0.5 select_reduce_fusion
  387.4 112.8 %all-to-all-done.1 = bf16[8,16,10,2048]{3,1,2,0:T(8,128)(2,1)} async-done(((bf16[8,16,10,2048]{3,1,2,0:T(8,128)(2,1)}), bf16[8,16,10,2048]{3,1,2,0:T(8,128)(2,1)}, u32[]{:S(2)}, u32[]{:S(2)}) %all-to-all-start.1) | async-done | bytes 5242912 | tf_op jit(solution)/shard_map/all_to_all | solution.py:124
  500.2 7.9 %copy.146 = f32[8,16,10,2048]{3,1,0,2:T(8,128)} copy(bf16[8,16,10,2048]{3,1,2,0:T(8,128)(2,1)} %all-to-all-done.1) | data formatting | bytes 15728640 | tf_op jit(solution)/shard_map/convert_element_type | solution.py:126
  508.1 12.9 %reshape.144 = f32[64,2,10,2048]{3,1,0,2:T(2,128)} reshape(f32[8,16,10,2048]{3,1,0,2:T(8,128)} %copy.146) | data formatting | bytes 20971520 | tf_op jit(solution)/shard_map/convert_element_type | solution.py:126
  521.0 16.9 %reduce_sum.88 = f32[64,10,2048]{2,0,1:T(8,128)} reduce(f32[64,2,10,2048]{3,1,0,2:T(2,128)} %reshape.144, f32[]{:T(128)} %constant.14.clone.1), dimensions={1}, to_apply=%region_14.15 | reduce | flops 1310720 | bytes 15728644 | tf_op jit(solution)/shard_map/reduce_sum | solution.py:126
  538.0 9.1 %copy.147 = f32[64,10,2048]{2,1,0:T(8,128)} copy(f32[64,10,2048]{2,0,1:T(8,128)} %reduce_sum.88) | data formatting | bytes 10485760 | tf_op jit(solution)/shard_map/reduce_sum | solution.py:126
  547.1 7.4 %reshape.143 = f32[640,2048]{1,0:T(8,128)} reshape(f32[64,10,2048]{2,1,0:T(8,128)} %copy.147) | data formatting | bytes 10485760 | tf_op jit(solution)/shard_map/reshape | solution.py:126
  554.5 6.4 %convolution_convert_fusion.2 = bf16[64,2048]{1,0:T(8,128)(2,1)} fusion(f32[64,640]{1,0:T(8,128)S(1)} %select_reduce_fusion, f32[640,2048]{1,0:T(8,128)} %reshape.143), kind=kOutput, calls=%fused_computation.6 | convolution fusion | flops 1006764032 | bytes 5668864 | tf_op jit(solution)/shard_map/dot_general | solution.py:129
  560.9 0.0 reduce-scatter.2.cloned.1.call-update
  560.9 18.8 %reduce-scatter.2.cloned.1.call-done = bf16[64,512]{1,0:T(8,128)(2,1)} async-done(((bf16[64,2048]{1,0:T(8,128)(2,1)}), bf16[64,512]{1,0:T(8,128)(2,1)}) %reduce-scatter.2.cloned.1.call-update) | async-done | bytes 65552 | tf_op jit(solution)/shard_map/reduce_scatter | solution.py:135
  579.8 1.5 add_convert_fusion
  (27 shorter events, 0.3 us)
Async XLA Ops:
  6.5 92.7 %copy-start = (bf16[512,2048]{1,0:T(8,128)(2,1)S(1)}, bf16[512,2048]{1,0:T(8,128)(2,1)}, u32[]{:S(2)}) copy-start(bf16[512,2048]{1,0:T(8,128)(2,1)} %param.25) | copy-start | bytes 6291460
  6.5 123.3 %all-reduce.3.cloned.1.call-start = ((), (), s32[]{:S(2)}) async-start(), calls=%async_computation.3 | async-start | bytes 524288 | tf_op jit(solution)/shard_map/psum | solution.py:92
  337.5 2.3 copy-start.3
  366.9 7.3 %copy-start.2 = (bf16[16,80,2048]{2,1,0:T(8,128)(2,1)S(1)}, bf16[16,80,2048]{2,1,0:T(8,128)(2,1)}, u32[]{:S(2)}) copy-start(bf16[16,80,2048]{2,1,0:T(8,128)(2,1)} %convolution_convert_fusion) | copy-start | bytes 15728644
  380.8 5.1 copy-start.4
  380.8 5.1 copy-start.5
  380.8 5.1 copy-start.6
  380.8 119.4 %all-to-all-start.1 = ((bf16[8,16,10,2048]{3,1,2,0:T(8,128)(2,1)}), bf16[8,16,10,2048]{3,1,2,0:T(8,128)(2,1)}, u32[]{:S(2)}, u32[]{:S(2)}) async-start(bf16[8,16,10,2048]{3,1,2,0:T(8,128)(2,1)} %copy.145), calls=%async_computation.1 | async-start | bytes 10485760 | tf_op jit(solution)/shard_map/all_to_all | solution.py:124
  385.6 194.1 %reduce-scatter.2.cloned.1.call-start = ((), (), s32[]{:S(2)}) async-start(), calls=%async_computation.4 | async-start | bytes 327680 | tf_op jit(solution)/shard_map/reduce_scatter | solution.py:135
  538.0 43.3 %copy-start.1 = (bf16[512,2048]{1,0:T(8,128)(2,1)S(1)}, bf16[512,2048]{1,0:T(8,128)(2,1)}, u32[]{:S(2)}) copy-start(bf16[512,2048]{1,0:T(8,128)(2,1)} %param.25) | copy-start | bytes 6291460
Sparse Core Ops, SparseCore 0:
  100.6 29.2 all-reduce.2
  561.0 18.6 reduce-scatter.1
